TPU v7x, 32 devices: a whole 2x2x4 slice. The times are simulated.
32 devices in a mesh: dp: 16 (over z, x, core), tensor: 2 (over y).
Axes of the slice: x: 2, y: 2, z: 4, core: 2. Of those that a mesh axis runs over, the one named last changes fastest.
Arguments:
- tokens: bfloat16 [32768, 1024], P(('dp', 'tensor')), may hold values from -6 to 6
- w_qkv: bfloat16 [1024, 3, 1024], P('dp', None, 'tensor'), may hold values from -0.1875 to 0.1875
- w_out: bfloat16 [1024, 1024], P('tensor', 'dp'), may hold values from -0.75 to 0.75
- w_up: bfloat16 [1024, 4096], P('dp', 'tensor'), may hold values from -0.1875 to 0.1875
- w_down: bfloat16 [4096, 1024], P('tensor', 'dp'), may hold values from -0.09375 to 0.09375
- ln1_gain: float32 [1024], replicated, may hold values from 0.5 to 1.5
- ln1_bias: float32 [1024], replicated, may hold values from -1.5 to 1.5
- ln2_gain: float32 [1024], replicated, may hold values from 0.5 to 1.5
- ln2_bias: float32 [1024], replicated, may hold values from -1.5 to 1.5
- a_qkv: bfloat16 [8, 1024, 16], replicated, may hold values from -0.1875 to 0.1875
- b_qkv: bfloat16 [8, 16, 3, 1024], P(None, None, None, 'tensor'), may hold values from -0.75 to 0.75
- a_out: bfloat16 [8, 1024, 16], P(None, 'tensor'), may hold values from -0.75 to 0.75
- b_out: bfloat16 [8, 16, 1024], replicated, may hold values from -0.75 to 0.75
- a_up: bfloat16 [8, 1024, 16], replicated, may hold values from -0.1875 to 0.1875
- b_up: bfloat16 [8, 16, 4096], P(None, None, 'tensor'), may hold values from -0.75 to 0.75
- a_down: bfloat16 [8, 4096, 16], P(None, 'tensor'), may hold values from -0.09375 to 0.09375
- b_down: bfloat16 [8, 16, 1024], replicated, may hold values from -0.75 to 0.75
- adapter_idx: int32 [16, 4], P('dp'), may hold values from 0 to 7
- pic_start: int32 [16, 2], P('dp'), may hold values from 0 to 1792, as said below
- cotangent: bfloat16 [32768, 1024], P(('dp', 'tensor')), may hold values from -6 to 6
Outputs:
- layer_out: bfloat16 [32768, 1024], P(('dp', 'tensor'))
- grad_tokens: float32 [32768, 1024], P(('dp', 'tensor'))
- grad_a_qkv: float32 [8, 1024, 16], replicated
- grad_b_qkv: float32 [8, 16, 3, 1024], P(None, None, None, 'tensor')
- grad_a_out: float32 [8, 1024, 16], P(None, 'tensor')
- grad_b_out: float32 [8, 16, 1024], replicated
- grad_a_up: float32 [8, 1024, 16], replicated
- grad_b_up: float32 [8, 16, 4096], P(None, None, 'tensor')
- grad_a_down: float32 [8, 4096, 16], P(None, 'tensor')
- grad_b_down: float32 [8, 16, 1024], replicated
Inputs may be any that keep to these rules, and one draw needn't show every extreme that they name: `pic_start`: each sequence has 2 picture spans of 256 tokens; span k starts between k * 1024 and (k + 1) * 1024 - 256, so spans never intersect.
All inputs are finite; a program needn't handle non-finite values.
Results may differ from a plain program's by a relative error of at most 0.014.
Values may be sent and summed in bfloat16 or wider, within the bound.
A program may use at most 320 MiB of HBM per device.

v0:
```python
import jax
import jax.numpy as jnp
from jax import lax
from jax.sharding import PartitionSpec as P

HD = 64
SPAN = 256
BLOCK = 512


def matmul(left, right):
    return jnp.dot(left, right, preferred_element_type=jnp.float32)


def contract_rows(left, right):
    return lax.dot_general(
        left, right, (((0,), (0,)), ((), ())), preferred_element_type=jnp.float32
    )


def against(left, right):
    return lax.dot_general(
        left, right, (((1,), (1,)), ((), ())), preferred_element_type=jnp.float32
    )


def layer_norm(values, multiplier, addend):
    center = values - jnp.mean(values, axis=-1, keepdims=True)
    spread = jnp.mean(center * center, axis=-1, keepdims=True)
    return center * lax.rsqrt(spread + 1e-05) * multiplier + addend


def span_labels(positions, starts):
    inside = (positions[:, None] >= starts[None, :]) & (positions[:, None] < starts[None, :] + SPAN)
    labels = jnp.arange(1, starts.shape[0] + 1, dtype=jnp.int32)
    return jnp.sum(jnp.where(inside, labels[None, :], 0), axis=1)


def allowed_mask(offset, row_count, length, starts):
    row_pos = offset + jnp.arange(row_count, dtype=jnp.int32)
    col_pos = jnp.arange(length, dtype=jnp.int32)
    row_span = span_labels(row_pos, starts)
    col_span = span_labels(col_pos, starts)
    causal = col_pos[None, :] <= row_pos[:, None]
    joined = (row_span[:, None] == col_span[None, :]) & (row_span[:, None] > 0)
    return causal | joined


def masked_scores(query_block, key_rows, offset, length, starts, factor):
    scores = (
        jnp.einsum("qhd,khd->hqk", query_block, key_rows, preferred_element_type=jnp.float32)
        * factor
    )
    allowed = allowed_mask(offset, BLOCK, length, starts)
    return jnp.where(allowed[None], scores, -1000000000.0)


def attend(queries, key_rows, value_rows, starts):
    length, heads, width = queries.shape
    factor = width ** (-0.5)

    def one_block(block_number):
        offset = block_number * BLOCK
        query_block = lax.dynamic_slice_in_dim(queries, offset, BLOCK, 0)
        scores = masked_scores(query_block, key_rows, offset, length, starts, factor)
        peak = jnp.max(scores, axis=-1, keepdims=True)
        raised = jnp.exp(scores - peak)
        totals = jnp.sum(raised, axis=-1, keepdims=True)
        weights_low = (raised / totals).astype(jnp.bfloat16)
        blended = jnp.einsum(
            "hqk,khd->qhd", weights_low, value_rows, preferred_element_type=jnp.float32
        )
        return (
            blended.astype(jnp.bfloat16).reshape(BLOCK, heads * width),
            (peak + jnp.log(totals))[..., 0],
        )

    blended, log_sums = lax.map(one_block, jnp.arange(length // BLOCK, dtype=jnp.int32))
    return (blended.reshape(length, heads * width), log_sums)


def attend_back(queries, key_rows, value_rows, grad_mix, log_sums, starts):
    length, heads, width = queries.shape
    factor = width ** (-0.5)

    def one_block(carry, inputs_pair):
        key_grad, value_grad = carry
        block_number, block_sums = inputs_pair
        offset = block_number * BLOCK
        query_block = lax.dynamic_slice_in_dim(queries, offset, BLOCK, 0)
        grad_block = lax.dynamic_slice_in_dim(grad_mix, offset, BLOCK, 0)
        scores = masked_scores(query_block, key_rows, offset, length, starts, factor)
        weights = jnp.exp(scores - block_sums[:, :, None])
        dots = jnp.einsum(
            "qhd,khd->hqk", grad_block, value_rows, preferred_element_type=jnp.float32
        )
        inner = jnp.sum(weights * dots, axis=-1, keepdims=True)
        slopes = (weights * (dots - inner) * factor).astype(jnp.bfloat16)
        query_grad = jnp.einsum(
            "hqk,khd->qhd", slopes, key_rows, preferred_element_type=jnp.float32
        )
        key_grad = key_grad + jnp.einsum(
            "hqk,qhd->khd", slopes, query_block, preferred_element_type=jnp.float32
        )
        value_grad = value_grad + jnp.einsum(
            "hqk,qhd->khd",
            weights.astype(jnp.bfloat16),
            grad_block,
            preferred_element_type=jnp.float32,
        )
        return ((key_grad, value_grad), query_grad)

    initial = jnp.zeros(key_rows.shape, jnp.float32)
    numbers = jnp.arange(length // BLOCK, dtype=jnp.int32)
    (key_grad, value_grad), query_grad = lax.scan(
        one_block, (initial, initial), (numbers, log_sums)
    )
    return (query_grad.reshape(length, heads, width), key_grad, value_grad)


def fetch_frozen(first, second):
    return (
        lax.all_gather(first, "dp", axis=0, tiled=True),
        lax.all_gather(second, "dp", axis=1, tiled=True),
    )


def enter_rows(normed, reduced):
    return (
        lax.all_gather(normed, "tensor", axis=0, tiled=True),
        lax.all_gather(reduced, "tensor", axis=0, tiled=True),
    )


def leave_rows(partial_value, reduced):
    return (
        lax.psum_scatter(partial_value, "tensor", scatter_dimension=0, tiled=True),
        lax.psum_scatter(reduced, "tensor", scatter_dimension=0, tiled=True),
    )


def enter_grads(branch, reduced):
    return (
        lax.all_gather(branch, "tensor", axis=0, tiled=True),
        lax.all_gather(reduced, "tensor", axis=0, tiled=True),
    )


def leave_grads(partial_value, reduced):
    return (
        lax.psum_scatter(partial_value, "tensor", scatter_dimension=0, tiled=True),
        lax.psum_scatter(reduced, "tensor", scatter_dimension=0, tiled=True),
    )


def per_device(
    tokens,
    w_qkv,
    w_out,
    w_up,
    w_down,
    ln1_gain,
    ln1_bias,
    ln2_gain,
    ln2_bias,
    a_qkv,
    b_qkv,
    a_out,
    b_out,
    a_up,
    b_up,
    a_down,
    b_down,
    adapter_idx,
    pic_start,
    cotangent,
):
    selection = adapter_idx[0]
    starts = pic_start[0]

    def chosen(stacked, which_one):
        return lax.dynamic_index_in_dim(stacked, selection[which_one], 0, keepdims=False)

    low_qkv_in = chosen(a_qkv, 0)
    rank = low_qkv_in.shape[1]
    low_qkv_out = chosen(b_qkv, 0).reshape(rank, -1)
    low_out_in = chosen(a_out, 1)
    low_out_out = chosen(b_out, 1)
    low_up_in = chosen(a_up, 2)
    low_up_out = chosen(b_up, 2)
    low_down_in = chosen(a_down, 3)
    low_down_out = chosen(b_down, 3)
    heads_here = low_out_in.shape[0] // HD

    def run_forward(own_tokens, frozen):
        qkv_rows, out_rows, up_rows, down_rows = frozen
        qkv_full, out_full = fetch_frozen(qkv_rows, out_rows)
        qkv_flat = qkv_full.reshape(qkv_full.shape[0], -1)
        own_float = own_tokens.astype(jnp.float32)
        normed = layer_norm(own_float, ln1_gain, ln1_bias).astype(jnp.bfloat16)
        reduced = matmul(normed, low_qkv_in).astype(jnp.bfloat16)
        normed_all, reduced_all = enter_rows(normed, reduced)
        length = normed_all.shape[0]
        project = (matmul(normed_all, qkv_flat) + matmul(reduced_all, low_qkv_out)).astype(
            jnp.bfloat16
        )
        split = project.reshape(length, 3, heads_here, HD)
        blended, log_sums = attend(split[:, 0], split[:, 1], split[:, 2], starts)
        main_part, low_part = leave_rows(matmul(blended, out_full), matmul(blended, low_out_in))
        low_out_val = low_part.astype(jnp.bfloat16)
        residual = own_float + main_part + matmul(low_out_val, low_out_out)
        up_full, down_full = fetch_frozen(up_rows, down_rows)
        normed_two = layer_norm(residual, ln2_gain, ln2_bias).astype(jnp.bfloat16)
        reduced_two = matmul(normed_two, low_up_in).astype(jnp.bfloat16)
        normed_two_all, reduced_two_all = enter_rows(normed_two, reduced_two)
        pre_act = matmul(normed_two_all, up_full) + matmul(reduced_two_all, low_up_out)
        hidden = jax.nn.gelu(pre_act, approximate=True).astype(jnp.bfloat16)
        main_two, low_two = leave_rows(matmul(hidden, down_full), matmul(hidden, low_down_in))
        low_down_val = low_two.astype(jnp.bfloat16)
        output = residual + main_two + matmul(low_down_val, low_down_out)
        kept_state = (
            qkv_flat,
            out_full,
            up_full,
            down_full,
            normed,
            reduced_all,
            split,
            blended,
            log_sums,
            low_out_val,
            residual,
            normed_two,
            reduced_two_all,
            pre_act,
            hidden,
            low_down_val,
        )
        return (output, kept_state)

    frozen = (w_qkv, w_out, w_up, w_down)
    output, kept_state = run_forward(tokens, frozen)
    fresh_tokens, fresh_frozen = lax.optimization_barrier((tokens, frozen))
    repeat_out, kept_state = run_forward(fresh_tokens, fresh_frozen)
    (
        qkv_flat,
        out_full,
        up_full,
        down_full,
        normed,
        reduced_all,
        split,
        blended,
        log_sums,
        low_out_val,
        residual,
        normed_two,
        reduced_two_all,
        pre_act,
        hidden,
        low_down_val,
    ) = kept_state
    cot_float = cotangent.astype(jnp.float32)
    grad_low_down = against(cotangent, low_down_out).astype(jnp.bfloat16)
    grad_b_down_here = contract_rows(low_down_val, cotangent)
    cot_all, grad_low_down_all = enter_grads(cotangent, grad_low_down)
    grad_hidden = against(cot_all, down_full) + against(grad_low_down_all, low_down_in)
    grad_a_down_here = contract_rows(hidden, grad_low_down_all)
    gelu_pull = jax.vjp(lambda inner_val: jax.nn.gelu(inner_val, approximate=True), pre_act)[1]
    grad_pre = gelu_pull(grad_hidden)[0].astype(jnp.bfloat16)
    grad_b_up_here = contract_rows(reduced_two_all, grad_pre)
    grad_normed_two, grad_reduced_two = leave_grads(
        against(grad_pre, up_full), against(grad_pre, low_up_out)
    )
    grad_low_up = grad_reduced_two.astype(jnp.bfloat16)
    grad_a_up_here = contract_rows(normed_two, grad_low_up)
    grad_normed_two = grad_normed_two + against(grad_low_up, low_up_in)
    norm_pull_two = jax.vjp(lambda inner_val: layer_norm(inner_val, ln2_gain, ln2_bias), residual)[
        1
    ]
    grad_resid = cot_float + norm_pull_two(grad_normed_two)[0]
    branch_low = grad_resid.astype(jnp.bfloat16)
    grad_low_out = against(branch_low, low_out_out).astype(jnp.bfloat16)
    grad_b_out_here = contract_rows(low_out_val, branch_low)
    branch_all, grad_low_out_all = enter_grads(branch_low, grad_low_out)
    grad_mix = (against(branch_all, out_full) + against(grad_low_out_all, low_out_in)).astype(
        jnp.bfloat16
    )
    grad_a_out_here = contract_rows(blended, grad_low_out_all)
    length = grad_mix.shape[0]
    query_grad, key_grad, value_grad = attend_back(
        split[:, 0],
        split[:, 1],
        split[:, 2],
        grad_mix.reshape(length, heads_here, HD),
        log_sums,
        starts,
    )
    grad_qkv = (
        jnp.stack([query_grad, key_grad, value_grad], axis=1)
        .reshape(length, -1)
        .astype(jnp.bfloat16)
    )
    grad_b_qkv_here = contract_rows(reduced_all, grad_qkv)
    grad_normed_one, grad_reduced_one = leave_grads(
        against(grad_qkv, qkv_flat), against(grad_qkv, low_qkv_out)
    )
    grad_low_qkv = grad_reduced_one.astype(jnp.bfloat16)
    grad_a_qkv_here = contract_rows(normed, grad_low_qkv)
    grad_normed_one = grad_normed_one + against(grad_low_qkv, low_qkv_in)
    norm_pull_one = jax.vjp(
        lambda inner_val: layer_norm(inner_val, ln1_gain, ln1_bias), tokens.astype(jnp.float32)
    )[1]
    grad_input = grad_resid + norm_pull_one(grad_normed_one)[0]
    slots = a_qkv.shape[0]

    def spread(gradient, which_one):
        onehot = (jnp.arange(slots, dtype=jnp.int32) == selection[which_one]).astype(jnp.float32)
        return onehot.reshape((slots,) + (1,) * gradient.ndim) * gradient[None]

    sharded = (
        lax.psum(spread(grad_b_qkv_here.reshape(rank, 3, -1), 0).astype(jnp.bfloat16), "dp").astype(
            jnp.float32
        ),
        lax.psum(spread(grad_a_out_here, 1).astype(jnp.bfloat16), "dp").astype(jnp.float32),
        lax.psum(spread(grad_b_up_here, 2).astype(jnp.bfloat16), "dp").astype(jnp.float32),
        lax.psum(spread(grad_a_down_here, 3).astype(jnp.bfloat16), "dp").astype(jnp.float32),
    )
    shared = lax.psum(
        (
            spread(grad_a_qkv_here, 0),
            spread(grad_b_out_here, 1),
            spread(grad_a_up_here, 2),
            spread(grad_b_down_here, 3),
        ),
        ("dp", "tensor"),
    )
    return (
        output.astype(jnp.bfloat16),
        grad_input,
        shared[0],
        sharded[0],
        sharded[1],
        shared[1],
        shared[2],
        sharded[2],
        sharded[3],
        shared[3],
    )


def solution(mesh):
    placed = (
        P(("dp", "tensor"), None),
        P("dp", None, "tensor"),
        P("tensor", "dp"),
        P("dp", "tensor"),
        P("tensor", "dp"),
        P(),
        P(),
        P(),
        P(),
        P(),
        P(None, None, None, "tensor"),
        P(None, "tensor", None),
        P(),
        P(),
        P(None, None, "tensor"),
        P(None, "tensor", None),
        P(),
        P("dp", None),
        P("dp", None),
        P(("dp", "tensor"), None),
    )
    return jax.shard_map(
        per_device,
        mesh=mesh,
        in_specs=placed,
        out_specs=(
            P(("dp", "tensor"), None),
            P(("dp", "tensor"), None),
            P(),
            P(None, None, None, "tensor"),
            P(None, "tensor", None),
            P(),
            P(),
            P(None, None, "tensor"),
            P(None, "tensor", None),
            P(),
        ),
        check_vma=False,
    )
```

profile of v0, /device:TPU:0, one launch (start us, length us, event | category | flops | bytes accessed | tf_op | source)
XLA Modules:
  0.0 2569.9 jit_solution(11967599070437223480)
XLA Ops:
  28.3 30.2 %all-gather.33.cloned.1.call-done = bf16[1024,3,512]{2,0,1:T(8,128)(2,1)} async-done(((bf16[64,3,512]{2,0,1:T(8,128)(2,1)}), bf16[1024,3,512]{2,0,1:T(8,128)(2,1)}) %all-gather.33.cloned.1.call-update) | async-done | bytes 3145744 | tf_op jit(solution)/shard_map/all_gather | solution.py:123
  63.1 52.4 %all-gather.31.cloned.1.call-done = bf16[2048,1024]{1,0:T(8,128)(2,1)} async-done(((bf16[1024,1024]{1,0:T(8,128)(2,1)}), bf16[2048,1024]{1,0:T(8,128)(2,1)}) %all-gather.31.cloned.1.call-update) | async-done | bytes 4194320 | tf_op jit(solution)/shard_map/all_gather | solution.py:130
  131.2 196.8 %while.38 = (s32[]{:T(128)}, bf16[4,512,512]{2,1,0:T(8,128)(2,1)}, f32[4,8,512]{2,1,0:T(8,128)S(1)}, s32[4]{0:T(128)S(1)}, s32[1,2]{1,0:T(1,128)S(1)}, /*index=5...) while((s32[]{:T(128)}, bf16[4,512,512]{2,1,0:T(8,128)(2,1)}, ...), condition=%wide.region_21.22_spmd, body=%wide.region_16.21_spmd.sunk | while | flops 2252623360 | bytes 112358664 | solution.py:78
  341.6 101.4 %reduce-scatter.20.cloned.1.call-done = f32[1024,1024]{1,0:T(8,128)} async-done(((f32[2048,1024]{1,0:T(8,128)}), f32[1024,1024]{1,0:T(8,128)}) %reduce-scatter.20.cloned.1.call-update) | async-done | bytes 4194320 | tf_op jit(solution)/shard_map/reduce_scatter | solution.py:137
  476.4 19.6 all-gather.39.cloned.1.call-done
  496.0 56.9 %all-gather.37.cloned.1.call-done = bf16[2048,1024]{1,0:T(8,128)(2,1)} async-done(((bf16[1024,1024]{1,0:T(8,128)(2,1)}), bf16[2048,1024]{1,0:T(8,128)(2,1)}) %all-gather.37.cloned.1.call-update) | async-done | bytes 4194320 | tf_op jit(solution)/shard_map/all_gather | solution.py:130
  582.9 28.3 %all-gather.29.cloned.1.call-done = bf16[2048,1024]{1,0:T(8,128)(2,1)} async-done(((bf16[1024,1024]{1,0:T(8,128)(2,1)}), bf16[2048,1024]{1,0:T(8,128)(2,1)}) %all-gather.29.cloned.1.call-update) | async-done | bytes 4194320 | tf_op jit(solution)/shard_map/all_gather | solution.py:144
  611.2 53.0 %all-gather.27.cloned.1.call-done = bf16[2048,1024]{0,1:T(8,128)(2,1)} async-done(((bf16[2048,64]{0,1:T(8,128)(2,1)}), bf16[2048,1024]{0,1:T(8,128)(2,1)}) %all-gather.27.cloned.1.call-update) | async-done | bytes 4194320 | tf_op jit(solution)/shard_map/all_gather | solution.py:124
  664.2 24.6 fusion.78
  709.8 97.8 %reduce-scatter.24.cloned.1.call-done = f32[1024,1024]{1,0:T(8,128)} async-done(((f32[2048,1024]{1,0:T(8,128)}), f32[1024,1024]{1,0:T(8,128)}) %reduce-scatter.24.cloned.1.call-update) | async-done | bytes 4194320 | tf_op jit(solution)/shard_map/reduce_scatter | solution.py:151
  825.0 49.9 %all-gather.41.cloned.1.call-done = bf16[2048,1024]{1,0:T(8,128)(2,1)} async-done(((bf16[1024,1024]{1,0:T(8,128)(2,1)}), bf16[2048,1024]{1,0:T(8,128)(2,1)}) %all-gather.41.cloned.1.call-update) | async-done | bytes 4194320 | tf_op jit(solution)/shard_map/all_gather | solution.py:144
  882.6 636.9 %while.39 = (s32[]{:T(128)}, f32[2048,8,64]{0,2,1:T(8,128)}, f32[2048,8,64]{0,2,1:T(8,128)}, bf16[4,512,8,64]{1,0,3,2:T(4,128)(2,1)}, s32[4]{0:T(128)S(1)}, /*in...) while((s32[]{:T(128)}, f32[2048,8,64]{0,2,1:T(8,128)}, ...), condition=%wide.region_34.35_spmd.clone, body=%wide.region_30.34_spmd.clone.sunk | while | flops 5494574592 | bytes 331953440 | solution.py:115
  932.6 42.6 %fusion.336 = bf16[1,512,8,64]{1,3,2,0:T(8,128)(2,1)S(1)} fusion(bf16[2048,8,64]{0,2,1:T(8,128)(2,1)} %get-tuple-element.550, f32[8,512,2048]{2,1,0:T(8,128)} %subtract_exponential_fusion.4, f32[8,512,2048]{2,1,0:T(8,128)} %fusion.335), kind=kOutput, calls=%fused_computation.66.clone.1 | convolution fusion | flops 1115691008 | bytes 69730304 | tf_op jit(solution)/shard_map/while/body/eval_jaxpr/hqk,khd->qhd/dot_general | solution.py:99
  975.2 43.4 %bitcast_add_fusion.5 = f32[2048,8,64]{0,2,1:T(8,128)} fusion(f32[2048,8,64]{0,2,1:T(8,128)} %get-tuple-element.529, f32[8,512,2048]{2,1,0:T(8,128)} %subtract_exponential_fusion.4, f32[8,512,2048]{2,1,0:T(8,128)} %fusion.335, pred[]{:T(512)S(6)} %compare.3, bf16[2048,8,64]{0,2,1:T(8,128)(2,1)} %get-tuple-element.548, s32[]{:T(128)S(6)} %select_n.138), kind=kOutput, calls=%fused_computation.63.clone.1 | convolution fusion | flops 1117788160 | bytes 143130624 | tf_op jit(solution)/shard_map/while/body/eval_jaxpr/hqk,qhd->khd/dot_general | solution.py:102
  1020.4 19.5 dynamic_update_slice.26
  1091.2 42.6 %fusion.336 = bf16[1,512,8,64]{1,3,2,0:T(8,128)(2,1)S(1)} fusion(bf16[2048,8,64]{0,2,1:T(8,128)(2,1)} %get-tuple-element.550, f32[8,512,2048]{2,1,0:T(8,128)} %subtract_exponential_fusion.4, f32[8,512,2048]{2,1,0:T(8,128)} %fusion.335), kind=kOutput, calls=%fused_computation.66.clone.1 | convolution fusion | flops 1115691008 | bytes 69730304 | tf_op jit(solution)/shard_map/while/body/eval_jaxpr/hqk,khd->qhd/dot_general | solution.py:99
  1133.7 44.6 %bitcast_add_fusion.5 = f32[2048,8,64]{0,2,1:T(8,128)} fusion(f32[2048,8,64]{0,2,1:T(8,128)} %get-tuple-element.529, f32[8,512,2048]{2,1,0:T(8,128)} %subtract_exponential_fusion.4, f32[8,512,2048]{2,1,0:T(8,128)} %fusion.335, pred[]{:T(512)S(6)} %compare.3, bf16[2048,8,64]{0,2,1:T(8,128)(2,1)} %get-tuple-element.548, s32[]{:T(128)S(6)} %select_n.138), kind=kOutput, calls=%fused_computation.63.clone.1 | convolution fusion | flops 1117788160 | bytes 143130624 | tf_op jit(solution)/shard_map/while/body/eval_jaxpr/hqk,qhd->khd/dot_general | solution.py:102
  1180.2 19.5 dynamic_update_slice.26
  1250.9 42.6 %fusion.336 = bf16[1,512,8,64]{1,3,2,0:T(8,128)(2,1)S(1)} fusion(bf16[2048,8,64]{0,2,1:T(8,128)(2,1)} %get-tuple-element.550, f32[8,512,2048]{2,1,0:T(8,128)} %subtract_exponential_fusion.4, f32[8,512,2048]{2,1,0:T(8,128)} %fusion.335), kind=kOutput, calls=%fused_computation.66.clone.1 | convolution fusion | flops 1115691008 | bytes 69730304 | tf_op jit(solution)/shard_map/while/body/eval_jaxpr/hqk,khd->qhd/dot_general | solution.py:99
  1293.4 44.6 %bitcast_add_fusion.5 = f32[2048,8,64]{0,2,1:T(8,128)} fusion(f32[2048,8,64]{0,2,1:T(8,128)} %get-tuple-element.529, f32[8,512,2048]{2,1,0:T(8,128)} %subtract_exponential_fusion.4, f32[8,512,2048]{2,1,0:T(8,128)} %fusion.335, pred[]{:T(512)S(6)} %compare.3, bf16[2048,8,64]{0,2,1:T(8,128)(2,1)} %get-tuple-element.548, s32[]{:T(128)S(6)} %select_n.138), kind=kOutput, calls=%fused_computation.63.clone.1 | convolution fusion | flops 1117788160 | bytes 143130624 | tf_op jit(solution)/shard_map/while/body/eval_jaxpr/hqk,qhd->khd/dot_general | solution.py:102
  1410.7 42.6 %fusion.336 = bf16[1,512,8,64]{1,3,2,0:T(8,128)(2,1)S(1)} fusion(bf16[2048,8,64]{0,2,1:T(8,128)(2,1)} %get-tuple-element.550, f32[8,512,2048]{2,1,0:T(8,128)} %subtract_exponential_fusion.4, f32[8,512,2048]{2,1,0:T(8,128)} %fusion.335), kind=kOutput, calls=%fused_computation.66.clone.1 | convolution fusion | flops 1115691008 | bytes 69730304 | tf_op jit(solution)/shard_map/while/body/eval_jaxpr/hqk,khd->qhd/dot_general | solution.py:99
  1453.3 44.6 %bitcast_add_fusion.5 = f32[2048,8,64]{0,2,1:T(8,128)} fusion(f32[2048,8,64]{0,2,1:T(8,128)} %get-tuple-element.529, f32[8,512,2048]{2,1,0:T(8,128)} %subtract_exponential_fusion.4, f32[8,512,2048]{2,1,0:T(8,128)} %fusion.335, pred[]{:T(512)S(6)} %compare.3, bf16[2048,8,64]{0,2,1:T(8,128)(2,1)} %get-tuple-element.548, s32[]{:T(128)S(6)} %select_n.138), kind=kOutput, calls=%fused_computation.63.clone.1 | convolution fusion | flops 1117788160 | bytes 143130624 | tf_op jit(solution)/shard_map/while/body/eval_jaxpr/hqk,qhd->khd/dot_general | solution.py:102
  1545.5 98.0 %reduce-scatter.28.cloned.1.call-done = f32[1024,1024]{1,0:T(8,128)} async-done(((f32[2048,1024]{1,0:T(8,128)}), f32[1024,1024]{1,0:T(8,128)}) %reduce-scatter.28.cloned.1.call-update) | async-done | bytes 4194320 | tf_op jit(solution)/shard_map/reduce_scatter | solution.py:151
  1654.6 36.3 %all-gather.17.cloned.1.call-done = bf16[1024,3,512]{2,0,1:T(8,128)(2,1)} async-done(((bf16[64,3,512]{2,0,1:T(8,128)(2,1)}), bf16[1024,3,512]{2,0,1:T(8,128)(2,1)}) %all-gather.17.cloned.1.call-update) | async-done | bytes 3145744 | tf_op jit(solution)/shard_map/all_gather | solution.py:123
  1701.6 47.1 %all-gather.15.cloned.1.call-done = bf16[2048,1024]{1,0:T(8,128)(2,1)} async-done(((bf16[1024,1024]{1,0:T(8,128)(2,1)}), bf16[2048,1024]{1,0:T(8,128)(2,1)}) %all-gather.15.cloned.1.call-update) | async-done | bytes 4194320 | tf_op jit(solution)/shard_map/all_gather | solution.py:130
  1764.3 144.6 %while.37 = (s32[]{:T(128)}, bf16[4,512,512]{2,1,0:T(8,128)(2,1)}, s32[4]{0:T(128)S(1)}, s32[1,2]{1,0:T(1,128)S(1)}, bf16[2048,8,64]{0,2,1:T(8,128)(2,1)}, /*ind...) while((s32[]{:T(128)}, bf16[4,512,512]{2,1,0:T(8,128)(2,1)}, ...), condition=%wide.region_7.8_spmd, body=%wide.region_2.7_spmd.sunk | while | flops 2202297856 | bytes 76608768 | solution.py:78
  1922.2 101.7 %reduce-scatter.12.cloned.1.call-done = f32[1024,1024]{1,0:T(8,128)} async-done(((f32[2048,1024]{1,0:T(8,128)}), f32[1024,1024]{1,0:T(8,128)}) %reduce-scatter.12.cloned.1.call-update) | async-done | bytes 4194320 | tf_op jit(solution)/shard_map/reduce_scatter | solution.py:137
  2076.5 57.3 %all-gather.21.cloned.1.call-done = bf16[2048,1024]{1,0:T(8,128)(2,1)} async-done(((bf16[1024,1024]{1,0:T(8,128)(2,1)}), bf16[2048,1024]{1,0:T(8,128)(2,1)}) %all-gather.21.cloned.1.call-update) | async-done | bytes 4194320 | tf_op jit(solution)/shard_map/all_gather | solution.py:130
  2166.0 20.7 all-gather.25.cloned.1.call-done
  2210.7 88.6 %all-reduce.7.cloned.1.call-done = (bf16[8,16,3,512]{3,1,2,0:T(8,128)(2,1)}, bf16[8,512,16]{1,2,0:T(8,128)(2,1)}, bf16[8,16,2048]{2,1,0:T(8,128)(2,1)}, bf16[8,2048,16]{1,2,0:T(8,128)(2,1)}) async-done(((bf16[8,16,3,512]{3,1,2,0:T(8,128)(2,1)}, bf16[8,512,16]{1,2,0:T(8,128)(2,1)}, bf16[8,16,2048]{2,1,0:T(8,128)(2,1)}, bf16[8,2048,16]{1,2,0:T(8,128)(2,1)}), (bf16[8,16,3,512]{3,1,2,0:T(8,128)(2,1)}, ...) | async-done | bytes 1572880 | tf_op jit(solution)/shard_map/psum | solution.py:322
  2311.1 101.4 %reduce-scatter.16.cloned.1.call-done = f32[1024,1024]{1,0:T(8,128)} async-done(((f32[2048,1024]{1,0:T(8,128)}), f32[1024,1024]{1,0:T(8,128)}) %reduce-scatter.16.cloned.1.call-update) | async-done | bytes 4194320 | tf_op jit(solution)/shard_map/reduce_scatter | solution.py:137
  2418.1 136.9 %all-reduce.5.cloned.1.call-done = (f32[8,1024,16]{1,2,0:T(8,128)}, f32[8,16,1024]{2,1,0:T(8,128)}, f32[8,1024,16]{1,2,0:T(8,128)}, f32[8,16,1024]{2,1,0:T(8,128)}) async-done(((f32[8,1024,16]{1,2,0:T(8,128)}, f32[8,16,1024]{2,1,0:T(8,128)}, f32[8,1024,16]{1,2,0:T(8,128)}, f32[8,16,1024]{2,1,0:T(8,128)}), (f32[8,1024,16]{1,2,0:T(8,128)}, f32[8,16,1024]{2,1,0:T(8,128)}, f32[8,1024,16]{1,2,0:T(8,128)}, ...) | async-done | bytes 2097168 | tf_op jit(solution)/shard_map/psum | solution.py:329
  (416 shorter events, 948.8 us)
Async XLA Ops:
  7.2 560.9 %copy-start = (bf16[8,16,2048]{2,1,0:T(8,128)(2,1)S(1)}, bf16[8,16,2048]{2,1,0:T(8,128)(2,1)}, u32[]{:S(2)}) copy-start(bf16[8,16,2048]{2,1,0:T(8,128)(2,1)} %param.40) | copy-start | bytes 1572868
  7.2 51.2 %all-gather.33.cloned.1.call-start = ((), (), s32[]{:S(2)}) async-start(), calls=%async_computation.24 | async-start | bytes 3342336 | tf_op jit(solution)/shard_map/all_gather | solution.py:123
  8.0 107.6 %all-gather.31.cloned.1.call-start = ((), (), s32[]{:S(2)}) async-start(), calls=%async_computation.23 | async-start | bytes 6291456 | tf_op jit(solution)/shard_map/all_gather | solution.py:130
  14.5 316.5 %all-gather.35.cloned.1.call-start = ((), (), s32[]{:S(2)}) async-start(), calls=%async_computation.25 | async-start | bytes 1114112 | tf_op jit(solution)/shard_map/all_gather | solution.py:124
  15.3 326.3 %reduce-scatter.22.cloned.1.call-start = ((), (), s32[]{:S(2)}) async-start(), calls=%async_computation.27 | async-start | bytes 196608 | tf_op jit(solution)/shard_map/reduce_scatter | solution.py:138
  19.9 105.2 %copy-start.25 = (bf16[2,8,3,512]{3,1,2,0:T(8,128)(2,1)}, bf16[2,8,3,512]{3,1,2,0:T(8,128)(2,1)S(1)}, u32[]{:S(2)}) copy-start(bf16[2,8,3,512]{3,1,2,0:T(8,128)(2,1)S(1)} %copy.91) | copy-start | bytes 147460
  331.0 112.0 %reduce-scatter.20.cloned.1.call-start = ((), (), s32[]{:S(2)}) async-start(), calls=%async_computation.26 | async-start | bytes 12582912 | tf_op jit(solution)/shard_map/reduce_scatter | solution.py:137
  338.6 104.4 %copy-start.2 = (bf16[1024,1024]{1,0:T(8,128)(2,1)S(1)}, bf16[1024,1024]{1,0:T(8,128)(2,1)}, u32[]{:S(2)}) copy-start(bf16[1024,1024]{1,0:T(8,128)(2,1)} %param.26) | copy-start | bytes 6291460
  338.6 157.3 %all-gather.39.cloned.1.call-start = ((), (), s32[]{:S(2)}) async-start(), calls=%async_computation.29 | async-start | bytes 4456448 | tf_op jit(solution)/shard_map/all_gather | solution.py:123
  339.2 213.6 %all-gather.37.cloned.1.call-start = ((), (), s32[]{:S(2)}) async-start(), calls=%async_computation.28 | async-start | bytes 6291456 | tf_op jit(solution)/shard_map/all_gather | solution.py:130
  450.1 161.1 %all-gather.29.cloned.1.call-start = ((), (), s32[]{:S(2)}) async-start(), calls=%async_computation.22 | async-start | bytes 6291456 | tf_op jit(solution)/shard_map/all_gather | solution.py:144
  450.9 213.3 %all-gather.27.cloned.1.call-start = ((), (), s32[]{:S(2)}) async-start(), calls=%async_computation.21 | async-start | bytes 4456448 | tf_op jit(solution)/shard_map/all_gather | solution.py:124
  451.6 258.2 %reduce-scatter.26.cloned.1.call-start = ((), (), s32[]{:S(2)}) async-start(), calls=%async_computation.31 | async-start | bytes 196608 | tf_op jit(solution)/shard_map/reduce_scatter | solution.py:152
  695.1 112.6 %reduce-scatter.24.cloned.1.call-start = ((), (), s32[]{:S(2)}) async-start(), calls=%async_computation.30 | async-start | bytes 12582912 | tf_op jit(solution)/shard_map/reduce_scatter | solution.py:151
  709.7 165.1 %all-gather.41.cloned.1.call-start = ((), (), s32[]{:S(2)}) async-start(), calls=%async_computation.32 | async-start | bytes 6291456 | tf_op jit(solution)/shard_map/all_gather | solution.py:144
  818.0 727.5 %reduce-scatter.30.cloned.1.call-start = ((), (), s32[]{:S(2)}) async-start(), calls=%async_computation.34 | async-start | bytes 196608 | tf_op jit(solution)/shard_map/reduce_scatter | solution.py:152
  1531.6 111.9 %reduce-scatter.28.cloned.1.call-start = ((), (), s32[]{:S(2)}) async-start(), calls=%async_computation.33 | async-start | bytes 12582912 | tf_op jit(solution)/shard_map/reduce_scatter | solution.py:151
  1543.5 99.9 %copy-start.42 = (f32[1024]{0:T(1024)S(1)}, f32[1024]{0:T(1024)}, u32[]{:S(2)}) copy-start(f32[1024]{0:T(1024)} %param.31) | copy-start | bytes 12292
  1543.5 147.4 %all-gather.17.cloned.1.call-start = ((), (), s32[]{:S(2)}) async-start(), calls=%async_computation.12 | async-start | bytes 3342336 | tf_op jit(solution)/shard_map/all_gather | solution.py:123
  1544.1 204.6 %all-gather.15.cloned.1.call-start = ((), (), s32[]{:S(2)}) async-start(), calls=%async_computation.11 | async-start | bytes 6291456 | tf_op jit(solution)/shard_map/all_gather | solution.py:130
  1654.0 257.9 %all-gather.19.cloned.1.call-start = ((), (), s32[]{:S(2)}) async-start(), calls=%async_computation.13 | async-start | bytes 1114112 | tf_op jit(solution)/shard_map/all_gather | solution.py:124
  1654.6 267.6 %reduce-scatter.14.cloned.1.call-start = ((), (), s32[]{:S(2)}) async-start(), calls=%async_computation.15 | async-start | bytes 196608 | tf_op jit(solution)/shard_map/reduce_scatter | solution.py:138
  1911.9 112.0 %reduce-scatter.12.cloned.1.call-start = ((), (), s32[]{:S(2)}) async-start(), calls=%async_computation.14 | async-start | bytes 12582912 | tf_op jit(solution)/shard_map/reduce_scatter | solution.py:137
  1919.5 104.4 %copy-start.4 = (bf16[1024,1024]{1,0:T(8,128)(2,1)S(1)}, bf16[1024,1024]{1,0:T(8,128)(2,1)}, u32[]{:S(2)}) copy-start(bf16[1024,1024]{1,0:T(8,128)(2,1)} %param.26) | copy-start | bytes 6291460
  1919.5 157.0 %all-gather.23.cloned.1.call-start = ((), (), s32[]{:S(2)}) async-start(), calls=%async_computation.17 | async-start | bytes 4456448 | tf_op jit(solution)/shard_map/all_gather | solution.py:123
  1920.1 213.8 %all-gather.21.cloned.1.call-start = ((), (), s32[]{:S(2)}) async-start(), calls=%async_computation.16 | async-start | bytes 6291456 | tf_op jit(solution)/shard_map/all_gather | solution.py:130
  2031.0 155.8 %all-gather.25.cloned.1.call-start = ((), (), s32[]{:S(2)}) async-start(), calls=%async_computation.18 | async-start | bytes 4456448 | tf_op jit(solution)/shard_map/all_gather | solution.py:124
  2031.8 169.7 %reduce-scatter.32.cloned.1.call-start = ((), (), s32[]{:S(2)}) async-start(), calls=%async_computation.35 | async-start | bytes 196608 | tf_op jit(solution)/shard_map/reduce_scatter | solution.py:138
  2050.0 249.2 %all-reduce.7.cloned.1.call-start = ((), (), s32[]{:S(2)}) async-start(), calls=%async_computation.37 | async-start | bytes 3145728 | tf_op jit(solution)/shard_map/psum | solution.py:322
  2058.6 252.5 %reduce-scatter.18.cloned.1.call-start = ((), (), s32[]{:S(2)}) async-start(), calls=%async_computation.20 | async-start | bytes 196608 | tf_op jit(solution)/shard_map/reduce_scatter | solution.py:138
  2165.7 246.9 %reduce-scatter.16.cloned.1.call-start = ((), (), s32[]{:S(2)}) async-start(), calls=%async_computation.19 | async-start | bytes 12582912 | tf_op jit(solution)/shard_map/reduce_scatter | solution.py:137
  2201.4 353.7 %all-reduce.5.cloned.1.call-start = ((), (), s32[]{:S(2)}) async-start(), calls=%async_computation.36 | async-start | bytes 4194304 | tf_op jit(solution)/shard_map/psum | solution.py:329
  (44 other events, 516.0 us)
Sparse Core Ops, SparseCore 0:
  10.2 48.1 all-gather.32
  60.0 55.5 all-gather.30
  117.7 37.9 all-gather.34
  331.1 10.3 reduce-scatter.21
  343.7 99.2 reduce-scatter.19
  445.2 50.6 all-gather.38
  497.6 55.2 all-gather.36
  554.5 56.7 all-gather.28
  613.6 50.5 all-gather.26
  695.2 8.7 reduce-scatter.25
  709.9 97.7 reduce-scatter.23
  818.1 56.7 all-gather.40
  1531.7 10.2 reduce-scatter.29
  1544.2 99.2 reduce-scatter.27
  1645.7 45.1 all-gather.16
  1693.0 55.6 all-gather.14
  1750.9 37.8 all-gather.18
  1912.0 10.1 reduce-scatter.13
  1924.6 99.2 reduce-scatter.11
  2025.8 50.6 all-gather.22
  2078.6 55.1 all-gather.20
  2136.0 50.7 all-gather.24
  2189.5 8.7 reduce-scatter.31
  2203.1 96.0 all-reduce.6
  2302.0 9.0 reduce-scatter.17
  2313.3 99.2 reduce-scatter.15
  2420.2 134.7 all-reduce.4
where the time goes:
time: 2580 us; the launch traced here: 2570 us
  waiting for transfers between devices  1200 us (47%)
  matrix products  1030 us (40%)
  local copies, waits for them, and re-layouts  148 us (6%)
  other arithmetic  123 us (5%)
  blocking collectives  28.7 us (1%)
    reduce_scatter x3, waiting for transfers between devices, leave_rows(): lax.psum_scatter(partial_value, 'tensor', scatter_dimension=0, tiled=True)  305 us
    all_gather x4, waiting for transfers between devices, enter_rows(): lax.all_gather(normed, 'tensor', axis=0, tiled=True)  214 us
    reduce_scatter x2, waiting for transfers between devices, leave_grads(): lax.psum_scatter(partial_value, 'tensor', scatter_dimension=0, tiled=True)  196 us
    dot_general x4, matrix products, one_block(): jnp.einsum('hqk,qhd->khd', slopes, query_block, preferred_element_type=jn...  177 us
    dot_general x4, matrix products, one_block(): jnp.einsum('hqk,khd->qhd', slopes, key_rows, preferred_element_type=jnp.f...  170 us
    dot_general x22, matrix products, matmul(): return jnp.dot(left, right, preferred_element_type=jnp.float32)  141 us
    psum x1, waiting for transfers between devices, per_device(): lax.psum((spread(grad_a_qkv_here, 0), spread(grad_b_out_here, 1), spread(...  137 us
    dot_general x8, matrix products, masked_scores(): jnp.einsum('qhd,khd->hqk', query_block, key_rows, preferred_element_type=...  129 us
  transfers between devices with their start and end apart: 27, of which 22 were waited for; matrix products, arithmetic and copies ran while one was open for 23% of the time, Pallas kernels for 0%

commit v1 on v0

--- a/solution.py
+++ b/solution.py
@@ -326,15 +326,14 @@
         lax.psum(spread(grad_b_up_here, 2).astype(jnp.bfloat16), "dp").astype(jnp.float32),
         lax.psum(spread(grad_a_down_here, 3).astype(jnp.bfloat16), "dp").astype(jnp.float32),
     )
-    shared = lax.psum(
-        (
-            spread(grad_a_qkv_here, 0),
-            spread(grad_b_out_here, 1),
-            spread(grad_a_up_here, 2),
-            spread(grad_b_down_here, 3),
-        ),
-        ("dp", "tensor"),
-    )
+    shared = (
+        spread(grad_a_qkv_here, 0),
+        spread(grad_b_out_here, 1),
+        spread(grad_a_up_here, 2),
+        spread(grad_b_down_here, 3),
+    )
+    for b in ("tensor", "dp"):
+        shared = jax.lax.psum(shared, b)
     return (
         output.astype(jnp.bfloat16),
         grad_input,

time: 2580 us -> 2610 us (1.012)
  waiting for transfers between devices: 1200 us -> 1230 us
    psum x1 -> x2, waiting for transfers between devices: 137 us -> 148 us  [per_device(): shared = jax.lax.psum(shared, b)]
  transfers between devices with their start and end apart: 27 -> 28, of which waited for: 22 -> 22; matrix products, arithmetic and copies ran while one was open for 23% -> 23% of each run, Pallas kernels for 0% -> 0%
where the time goes in v1:
time: 2610 us; the launch traced here: 2600 us
  waiting for transfers between devices  1230 us (47%)
  matrix products  1030 us (39%)
  local copies, waits for them, and re-layouts  147 us (6%)
  other arithmetic  123 us (5%)
  blocking collectives  28.7 us (1%)
    reduce_scatter x3, waiting for transfers between devices, leave_rows(): lax.psum_scatter(partial_value, 'tensor', scatter_dimension=0, tiled=True)  300 us
    all_gather x4, waiting for transfers between devices, enter_rows(): lax.all_gather(normed, 'tensor', axis=0, tiled=True)  214 us
    reduce_scatter x2, waiting for transfers between devices, leave_grads(): lax.psum_scatter(partial_value, 'tensor', scatter_dimension=0, tiled=True)  196 us
    dot_general x4, matrix products, one_block(): jnp.einsum('hqk,qhd->khd', slopes, query_block, preferred_element_type=jn...  177 us
    dot_general x4, matrix products, one_block(): jnp.einsum('hqk,khd->qhd', slopes, key_rows, preferred_element_type=jnp.f...  170 us
    psum x2, waiting for transfers between devices, per_device(): shared = jax.lax.psum(shared, b)  148 us
    dot_general x22, matrix products, matmul(): return jnp.dot(left, right, preferred_element_type=jnp.float32)  141 us
    dot_general x8, matrix products, masked_scores(): jnp.einsum('qhd,khd->hqk', query_block, key_rows, preferred_element_type=...  129 us
  transfers between devices with their start and end apart: 28, of which 22 were waited for; matrix products, arithmetic and copies ran while one was open for 23% of the time, Pallas kernels for 0%

profile of v1, /device:TPU:0, one launch (start us, length us, event | category | flops | bytes accessed | tf_op | source)
XLA Modules:
  0.0 2596.2 jit_solution(559693052840409561)
XLA Ops:
  28.4 29.8 %all-gather.33.cloned.1.call-done = bf16[1024,3,512]{2,0,1:T(8,128)(2,1)} async-done(((bf16[64,3,512]{2,0,1:T(8,128)(2,1)}), bf16[1024,3,512]{2,0,1:T(8,128)(2,1)}) %all-gather.33.cloned.1.call-update) | async-done | bytes 3145744 | tf_op jit(solution)/shard_map/all_gather | solution.py:123
  62.9 52.5 %all-gather.31.cloned.1.call-done = bf16[2048,1024]{1,0:T(8,128)(2,1)} async-done(((bf16[1024,1024]{1,0:T(8,128)(2,1)}), bf16[2048,1024]{1,0:T(8,128)(2,1)}) %all-gather.31.cloned.1.call-update) | async-done | bytes 4194320 | tf_op jit(solution)/shard_map/all_gather | solution.py:130
  131.0 196.6 %while.38 = (s32[]{:T(128)}, bf16[4,512,512]{2,1,0:T(8,128)(2,1)}, f32[4,8,512]{2,1,0:T(8,128)S(1)}, s32[4]{0:T(128)S(1)}, s32[1,2]{1,0:T(1,128)S(1)}, /*index=5...) while((s32[]{:T(128)}, bf16[4,512,512]{2,1,0:T(8,128)(2,1)}, ...), condition=%wide.region_21.22_spmd, body=%wide.region_16.21_spmd.sunk | while | flops 2252623360 | bytes 112358664 | solution.py:78
  341.0 101.4 %reduce-scatter.20.cloned.1.call-done = f32[1024,1024]{1,0:T(8,128)} async-done(((f32[2048,1024]{1,0:T(8,128)}), f32[1024,1024]{1,0:T(8,128)}) %reduce-scatter.20.cloned.1.call-update) | async-done | bytes 4194320 | tf_op jit(solution)/shard_map/reduce_scatter | solution.py:137
  495.4 56.9 %all-gather.37.cloned.1.call-done = bf16[2048,1024]{1,0:T(8,128)(2,1)} async-done(((bf16[1024,1024]{1,0:T(8,128)(2,1)}), bf16[2048,1024]{1,0:T(8,128)(2,1)}) %all-gather.37.cloned.1.call-update) | async-done | bytes 4194320 | tf_op jit(solution)/shard_map/all_gather | solution.py:130
  582.3 28.4 %all-gather.29.cloned.1.call-done = bf16[2048,1024]{1,0:T(8,128)(2,1)} async-done(((bf16[1024,1024]{1,0:T(8,128)(2,1)}), bf16[2048,1024]{1,0:T(8,128)(2,1)}) %all-gather.29.cloned.1.call-update) | async-done | bytes 4194320 | tf_op jit(solution)/shard_map/all_gather | solution.py:144
  610.7 53.0 %all-gather.27.cloned.1.call-done = bf16[2048,1024]{0,1:T(8,128)(2,1)} async-done(((bf16[2048,64]{0,1:T(8,128)(2,1)}), bf16[2048,1024]{0,1:T(8,128)(2,1)}) %all-gather.27.cloned.1.call-update) | async-done | bytes 4194320 | tf_op jit(solution)/shard_map/all_gather | solution.py:124
  663.7 24.3 fusion.78
  709.0 97.8 %reduce-scatter.24.cloned.1.call-done = f32[1024,1024]{1,0:T(8,128)} async-done(((f32[2048,1024]{1,0:T(8,128)}), f32[1024,1024]{1,0:T(8,128)}) %reduce-scatter.24.cloned.1.call-update) | async-done | bytes 4194320 | tf_op jit(solution)/shard_map/reduce_scatter | solution.py:151
  824.2 49.9 %all-gather.41.cloned.1.call-done = bf16[2048,1024]{1,0:T(8,128)(2,1)} async-done(((bf16[1024,1024]{1,0:T(8,128)(2,1)}), bf16[2048,1024]{1,0:T(8,128)(2,1)}) %all-gather.41.cloned.1.call-update) | async-done | bytes 4194320 | tf_op jit(solution)/shard_map/all_gather | solution.py:144
  881.9 636.6 %while.39 = (s32[]{:T(128)}, f32[2048,8,64]{0,2,1:T(8,128)}, f32[2048,8,64]{0,2,1:T(8,128)}, bf16[4,512,8,64]{1,0,3,2:T(4,128)(2,1)}, s32[4]{0:T(128)S(1)}, /*in...) while((s32[]{:T(128)}, f32[2048,8,64]{0,2,1:T(8,128)}, ...), condition=%wide.region_34.35_spmd.clone, body=%wide.region_30.34_spmd.clone.sunk | while | flops 5494574592 | bytes 331953440 | solution.py:115
  932.1 42.6 %fusion.336 = bf16[1,512,8,64]{1,3,2,0:T(8,128)(2,1)S(1)} fusion(bf16[2048,8,64]{0,2,1:T(8,128)(2,1)} %get-tuple-element.554, f32[8,512,2048]{2,1,0:T(8,128)} %subtract_exponential_fusion.4, f32[8,512,2048]{2,1,0:T(8,128)} %fusion.335), kind=kOutput, calls=%fused_computation.66.clone.1 | convolution fusion | flops 1115691008 | bytes 69730304 | tf_op jit(solution)/shard_map/while/body/eval_jaxpr/hqk,khd->qhd/dot_general | solution.py:99
  974.7 43.4 %bitcast_add_fusion.5 = f32[2048,8,64]{0,2,1:T(8,128)} fusion(f32[2048,8,64]{0,2,1:T(8,128)} %get-tuple-element.533, f32[8,512,2048]{2,1,0:T(8,128)} %subtract_exponential_fusion.4, f32[8,512,2048]{2,1,0:T(8,128)} %fusion.335, pred[]{:T(512)S(6)} %compare.3, bf16[2048,8,64]{0,2,1:T(8,128)(2,1)} %get-tuple-element.552, s32[]{:T(128)S(6)} %select_n.138), kind=kOutput, calls=%fused_computation.63.clone.1 | convolution fusion | flops 1117788160 | bytes 143130624 | tf_op jit(solution)/shard_map/while/body/eval_jaxpr/hqk,qhd->khd/dot_general | solution.py:102
  1019.9 19.5 dynamic_update_slice.26
  1090.5 42.6 %fusion.336 = bf16[1,512,8,64]{1,3,2,0:T(8,128)(2,1)S(1)} fusion(bf16[2048,8,64]{0,2,1:T(8,128)(2,1)} %get-tuple-element.554, f32[8,512,2048]{2,1,0:T(8,128)} %subtract_exponential_fusion.4, f32[8,512,2048]{2,1,0:T(8,128)} %fusion.335), kind=kOutput, calls=%fused_computation.66.clone.1 | convolution fusion | flops 1115691008 | bytes 69730304 | tf_op jit(solution)/shard_map/while/body/eval_jaxpr/hqk,khd->qhd/dot_general | solution.py:99
  1133.1 44.6 %bitcast_add_fusion.5 = f32[2048,8,64]{0,2,1:T(8,128)} fusion(f32[2048,8,64]{0,2,1:T(8,128)} %get-tuple-element.533, f32[8,512,2048]{2,1,0:T(8,128)} %subtract_exponential_fusion.4, f32[8,512,2048]{2,1,0:T(8,128)} %fusion.335, pred[]{:T(512)S(6)} %compare.3, bf16[2048,8,64]{0,2,1:T(8,128)(2,1)} %get-tuple-element.552, s32[]{:T(128)S(6)} %select_n.138), kind=kOutput, calls=%fused_computation.63.clone.1 | convolution fusion | flops 1117788160 | bytes 143130624 | tf_op jit(solution)/shard_map/while/body/eval_jaxpr/hqk,qhd->khd/dot_general | solution.py:102
  1250.1 42.6 %fusion.336 = bf16[1,512,8,64]{1,3,2,0:T(8,128)(2,1)S(1)} fusion(bf16[2048,8,64]{0,2,1:T(8,128)(2,1)} %get-tuple-element.554, f32[8,512,2048]{2,1,0:T(8,128)} %subtract_exponential_fusion.4, f32[8,512,2048]{2,1,0:T(8,128)} %fusion.335), kind=kOutput, calls=%fused_computation.66.clone.1 | convolution fusion | flops 1115691008 | bytes 69730304 | tf_op jit(solution)/shard_map/while/body/eval_jaxpr/hqk,khd->qhd/dot_general | solution.py:99
  1292.7 44.6 %bitcast_add_fusion.5 = f32[2048,8,64]{0,2,1:T(8,128)} fusion(f32[2048,8,64]{0,2,1:T(8,128)} %get-tuple-element.533, f32[8,512,2048]{2,1,0:T(8,128)} %subtract_exponential_fusion.4, f32[8,512,2048]{2,1,0:T(8,128)} %fusion.335, pred[]{:T(512)S(6)} %compare.3, bf16[2048,8,64]{0,2,1:T(8,128)(2,1)} %get-tuple-element.552, s32[]{:T(128)S(6)} %select_n.138), kind=kOutput, calls=%fused_computation.63.clone.1 | convolution fusion | flops 1117788160 | bytes 143130624 | tf_op jit(solution)/shard_map/while/body/eval_jaxpr/hqk,qhd->khd/dot_general | solution.py:102
  1409.8 42.6 %fusion.336 = bf16[1,512,8,64]{1,3,2,0:T(8,128)(2,1)S(1)} fusion(bf16[2048,8,64]{0,2,1:T(8,128)(2,1)} %get-tuple-element.554, f32[8,512,2048]{2,1,0:T(8,128)} %subtract_exponential_fusion.4, f32[8,512,2048]{2,1,0:T(8,128)} %fusion.335), kind=kOutput, calls=%fused_computation.66.clone.1 | convolution fusion | flops 1115691008 | bytes 69730304 | tf_op jit(solution)/shard_map/while/body/eval_jaxpr/hqk,khd->qhd/dot_general | solution.py:99
  1452.4 44.6 %bitcast_add_fusion.5 = f32[2048,8,64]{0,2,1:T(8,128)} fusion(f32[2048,8,64]{0,2,1:T(8,128)} %get-tuple-element.533, f32[8,512,2048]{2,1,0:T(8,128)} %subtract_exponential_fusion.4, f32[8,512,2048]{2,1,0:T(8,128)} %fusion.335, pred[]{:T(512)S(6)} %compare.3, bf16[2048,8,64]{0,2,1:T(8,128)(2,1)} %get-tuple-element.552, s32[]{:T(128)S(6)} %select_n.138), kind=kOutput, calls=%fused_computation.63.clone.1 | convolution fusion | flops 1117788160 | bytes 143130624 | tf_op jit(solution)/shard_map/while/body/eval_jaxpr/hqk,qhd->khd/dot_general | solution.py:102
  1544.4 98.0 %reduce-scatter.28.cloned.1.call-done = f32[1024,1024]{1,0:T(8,128)} async-done(((f32[2048,1024]{1,0:T(8,128)}), f32[1024,1024]{1,0:T(8,128)}) %reduce-scatter.28.cloned.1.call-update) | async-done | bytes 4194320 | tf_op jit(solution)/shard_map/reduce_scatter | solution.py:151
  1653.5 36.3 %all-gather.17.cloned.1.call-done = bf16[1024,3,512]{2,0,1:T(8,128)(2,1)} async-done(((bf16[64,3,512]{2,0,1:T(8,128)(2,1)}), bf16[1024,3,512]{2,0,1:T(8,128)(2,1)}) %all-gather.17.cloned.1.call-update) | async-done | bytes 3145744 | tf_op jit(solution)/shard_map/all_gather | solution.py:123
  1700.5 47.1 %all-gather.15.cloned.1.call-done = bf16[2048,1024]{1,0:T(8,128)(2,1)} async-done(((bf16[1024,1024]{1,0:T(8,128)(2,1)}), bf16[2048,1024]{1,0:T(8,128)(2,1)}) %all-gather.15.cloned.1.call-update) | async-done | bytes 4194320 | tf_op jit(solution)/shard_map/all_gather | solution.py:130
  1763.2 144.9 %while.37 = (s32[]{:T(128)}, bf16[4,512,512]{2,1,0:T(8,128)(2,1)}, s32[4]{0:T(128)S(1)}, s32[1,2]{1,0:T(1,128)S(1)}, bf16[2048,8,64]{0,2,1:T(8,128)(2,1)}, /*ind...) while((s32[]{:T(128)}, bf16[4,512,512]{2,1,0:T(8,128)(2,1)}, ...), condition=%wide.region_7.8_spmd, body=%wide.region_2.7_spmd.sunk | while | flops 2202297856 | bytes 76608768 | solution.py:78
  1926.1 96.8 %reduce-scatter.12.cloned.1.call-done = f32[1024,1024]{1,0:T(8,128)} async-done(((f32[2048,1024]{1,0:T(8,128)}), f32[1024,1024]{1,0:T(8,128)}) %reduce-scatter.12.cloned.1.call-update) | async-done | bytes 4194320 | tf_op jit(solution)/shard_map/reduce_scatter | solution.py:137
  2065.7 23.1 all-gather.23.cloned.1.call-done
  2088.8 57.4 %all-gather.21.cloned.1.call-done = bf16[2048,1024]{1,0:T(8,128)(2,1)} async-done(((bf16[1024,1024]{1,0:T(8,128)(2,1)}), bf16[2048,1024]{1,0:T(8,128)(2,1)}) %all-gather.21.cloned.1.call-update) | async-done | bytes 4194320 | tf_op jit(solution)/shard_map/all_gather | solution.py:130
  2178.3 20.7 all-gather.25.cloned.1.call-done
  2213.7 50.8 %all-reduce.9.cloned.1.call-done = (f32[8,1024,16]{1,2,0:T(8,128)}, f32[8,16,1024]{2,1,0:T(8,128)}, f32[8,1024,16]{1,2,0:T(8,128)}, f32[8,16,1024]{2,1,0:T(8,128)}) async-done(((f32[8,1024,16]{1,2,0:T(8,128)}, f32[8,16,1024]{2,1,0:T(8,128)}, f32[8,1024,16]{1,2,0:T(8,128)}, f32[8,16,1024]{2,1,0:T(8,128)}), (f32[8,1024,16]{1,2,0:T(8,128)}, f32[8,16,1024]{2,1,0:T(8,128)}, f32[8,1024,16]{1,2,0:T(8,128)}, ...) | async-done | bytes 2097168 | tf_op jit(solution)/shard_map/psum | solution.py:336
  2264.6 101.4 %all-reduce.11.cloned.1.call-done = (bf16[8,16,3,512]{3,1,2,0:T(8,128)(2,1)}, bf16[8,512,16]{1,2,0:T(8,128)(2,1)}, bf16[8,16,2048]{2,1,0:T(8,128)(2,1)}, bf16[8,2048,16]{1,2,0:T(8,128)(2,1)}) async-done(((bf16[8,16,3,512]{3,1,2,0:T(8,128)(2,1)}, bf16[8,512,16]{1,2,0:T(8,128)(2,1)}, bf16[8,16,2048]{2,1,0:T(8,128)(2,1)}, bf16[8,2048,16]{1,2,0:T(8,128)(2,1)}), (bf16[8,16,3,512]{3,1,2,0:T(8,128)(2,1)}, ...) | async-done | bytes 1572880 | tf_op jit(solution)/shard_map/psum | solution.py:322
  2377.8 101.5 %reduce-scatter.16.cloned.1.call-done = f32[1024,1024]{1,0:T(8,128)} async-done(((f32[2048,1024]{1,0:T(8,128)}), f32[1024,1024]{1,0:T(8,128)}) %reduce-scatter.16.cloned.1.call-update) | async-done | bytes 4194320 | tf_op jit(solution)/shard_map/reduce_scatter | solution.py:137
  2484.9 96.7 %all-reduce.7.cloned.1.call-done = (f32[8,1024,16]{1,2,0:T(8,128)}, f32[8,16,1024]{2,1,0:T(8,128)}, f32[8,1024,16]{1,2,0:T(8,128)}, f32[8,16,1024]{2,1,0:T(8,128)}) async-done(((f32[8,1024,16]{1,2,0:T(8,128)}, f32[8,16,1024]{2,1,0:T(8,128)}, f32[8,1024,16]{1,2,0:T(8,128)}, f32[8,16,1024]{2,1,0:T(8,128)}), (f32[8,1024,16]{1,2,0:T(8,128)}, f32[8,16,1024]{2,1,0:T(8,128)}, f32[8,1024,16]{1,2,0:T(8,128)}, ...) | async-done | bytes 2097168 | tf_op jit(solution)/shard_map/psum | solution.py:336
  (419 shorter events, 972.7 us)
Async XLA Ops:
  7.2 560.4 %copy-start = (bf16[8,16,2048]{2,1,0:T(8,128)(2,1)S(1)}, bf16[8,16,2048]{2,1,0:T(8,128)(2,1)}, u32[]{:S(2)}) copy-start(bf16[8,16,2048]{2,1,0:T(8,128)(2,1)} %param.40) | copy-start | bytes 1572868
  7.2 51.0 %all-gather.33.cloned.1.call-start = ((), (), s32[]{:S(2)}) async-start(), calls=%async_computation.24 | async-start | bytes 3342336 | tf_op jit(solution)/shard_map/all_gather | solution.py:123
  8.0 107.4 %all-gather.31.cloned.1.call-start = ((), (), s32[]{:S(2)}) async-start(), calls=%async_computation.23 | async-start | bytes 6291456 | tf_op jit(solution)/shard_map/all_gather | solution.py:130
  14.5 316.0 %all-gather.35.cloned.1.call-start = ((), (), s32[]{:S(2)}) async-start(), calls=%async_computation.25 | async-start | bytes 1114112 | tf_op jit(solution)/shard_map/all_gather | solution.py:124
  15.3 325.7 %reduce-scatter.22.cloned.1.call-start = ((), (), s32[]{:S(2)}) async-start(), calls=%async_computation.27 | async-start | bytes 196608 | tf_op jit(solution)/shard_map/reduce_scatter | solution.py:138
  20.0 104.9 %copy-start.25 = (bf16[2,8,3,512]{3,1,2,0:T(8,128)(2,1)}, bf16[2,8,3,512]{3,1,2,0:T(8,128)(2,1)S(1)}, u32[]{:S(2)}) copy-start(bf16[2,8,3,512]{3,1,2,0:T(8,128)(2,1)S(1)} %copy.91) | copy-start | bytes 147460
  330.5 111.9 %reduce-scatter.20.cloned.1.call-start = ((), (), s32[]{:S(2)}) async-start(), calls=%async_computation.26 | async-start | bytes 12582912 | tf_op jit(solution)/shard_map/reduce_scatter | solution.py:137
  338.1 104.3 %copy-start.2 = (bf16[1024,1024]{1,0:T(8,128)(2,1)S(1)}, bf16[1024,1024]{1,0:T(8,128)(2,1)}, u32[]{:S(2)}) copy-start(bf16[1024,1024]{1,0:T(8,128)(2,1)} %param.26) | copy-start | bytes 6291460
  338.1 157.3 %all-gather.39.cloned.1.call-start = ((), (), s32[]{:S(2)}) async-start(), calls=%async_computation.29 | async-start | bytes 4456448 | tf_op jit(solution)/shard_map/all_gather | solution.py:123
  338.7 213.6 %all-gather.37.cloned.1.call-start = ((), (), s32[]{:S(2)}) async-start(), calls=%async_computation.28 | async-start | bytes 6291456 | tf_op jit(solution)/shard_map/all_gather | solution.py:130
  449.6 161.1 %all-gather.29.cloned.1.call-start = ((), (), s32[]{:S(2)}) async-start(), calls=%async_computation.22 | async-start | bytes 6291456 | tf_op jit(solution)/shard_map/all_gather | solution.py:144
  450.3 213.3 %all-gather.27.cloned.1.call-start = ((), (), s32[]{:S(2)}) async-start(), calls=%async_computation.21 | async-start | bytes 4456448 | tf_op jit(solution)/shard_map/all_gather | solution.py:124
  451.1 258.0 %reduce-scatter.26.cloned.1.call-start = ((), (), s32[]{:S(2)}) async-start(), calls=%async_computation.31 | async-start | bytes 196608 | tf_op jit(solution)/shard_map/reduce_scatter | solution.py:152
  694.3 112.5 %reduce-scatter.24.cloned.1.call-start = ((), (), s32[]{:S(2)}) async-start(), calls=%async_computation.30 | async-start | bytes 12582912 | tf_op jit(solution)/shard_map/reduce_scatter | solution.py:151
  709.0 165.2 %all-gather.41.cloned.1.call-start = ((), (), s32[]{:S(2)}) async-start(), calls=%async_computation.32 | async-start | bytes 6291456 | tf_op jit(solution)/shard_map/all_gather | solution.py:144
  817.2 727.2 %reduce-scatter.30.cloned.1.call-start = ((), (), s32[]{:S(2)}) async-start(), calls=%async_computation.34 | async-start | bytes 196608 | tf_op jit(solution)/shard_map/reduce_scatter | solution.py:152
  1530.5 111.8 %reduce-scatter.28.cloned.1.call-start = ((), (), s32[]{:S(2)}) async-start(), calls=%async_computation.33 | async-start | bytes 12582912 | tf_op jit(solution)/shard_map/reduce_scatter | solution.py:151
  1542.5 147.4 %all-gather.17.cloned.1.call-start = ((), (), s32[]{:S(2)}) async-start(), calls=%async_computation.12 | async-start | bytes 3342336 | tf_op jit(solution)/shard_map/all_gather | solution.py:123
  1543.0 204.5 %all-gather.15.cloned.1.call-start = ((), (), s32[]{:S(2)}) async-start(), calls=%async_computation.11 | async-start | bytes 6291456 | tf_op jit(solution)/shard_map/all_gather | solution.py:130
  1652.9 258.1 %all-gather.19.cloned.1.call-start = ((), (), s32[]{:S(2)}) async-start(), calls=%async_computation.13 | async-start | bytes 1114112 | tf_op jit(solution)/shard_map/all_gather | solution.py:124
  1653.5 272.6 %reduce-scatter.14.cloned.1.call-start = ((), (), s32[]{:S(2)}) async-start(), calls=%async_computation.15 | async-start | bytes 196608 | tf_op jit(solution)/shard_map/reduce_scatter | solution.py:138
  1911.0 112.0 %reduce-scatter.12.cloned.1.call-start = ((), (), s32[]{:S(2)}) async-start(), calls=%async_computation.14 | async-start | bytes 12582912 | tf_op jit(solution)/shard_map/reduce_scatter | solution.py:137
  1918.6 124.3 %reduce-scatter.32.cloned.1.call-start = ((), (), s32[]{:S(2)}) async-start(), calls=%async_computation.35 | async-start | bytes 196608 | tf_op jit(solution)/shard_map/reduce_scatter | solution.py:138
  1918.8 104.2 %copy-start.4 = (bf16[1024,1024]{1,0:T(8,128)(2,1)S(1)}, bf16[1024,1024]{1,0:T(8,128)(2,1)}, u32[]{:S(2)}) copy-start(bf16[1024,1024]{1,0:T(8,128)(2,1)} %param.26) | copy-start | bytes 6291460
  1925.3 163.4 %all-gather.23.cloned.1.call-start = ((), (), s32[]{:S(2)}) async-start(), calls=%async_computation.17 | async-start | bytes 4456448 | tf_op jit(solution)/shard_map/all_gather | solution.py:123
  1926.1 220.1 %all-gather.21.cloned.1.call-start = ((), (), s32[]{:S(2)}) async-start(), calls=%async_computation.16 | async-start | bytes 6291456 | tf_op jit(solution)/shard_map/all_gather | solution.py:130
  2030.1 169.0 %all-gather.25.cloned.1.call-start = ((), (), s32[]{:S(2)}) async-start(), calls=%async_computation.18 | async-start | bytes 4456448 | tf_op jit(solution)/shard_map/all_gather | solution.py:124
  2030.8 233.7 %all-reduce.9.cloned.1.call-start = ((), (), s32[]{:S(2)}) async-start(), calls=%async_computation.37 | async-start | bytes 4194304 | tf_op jit(solution)/shard_map/psum | solution.py:336
  2050.7 315.2 %all-reduce.11.cloned.1.call-start = ((), (), s32[]{:S(2)}) async-start(), calls=%async_computation.38 | async-start | bytes 3145728 | tf_op jit(solution)/shard_map/psum | solution.py:322
  2059.4 318.4 %reduce-scatter.18.cloned.1.call-start = ((), (), s32[]{:S(2)}) async-start(), calls=%async_computation.20 | async-start | bytes 196608 | tf_op jit(solution)/shard_map/reduce_scatter | solution.py:138
  2178.0 301.3 %reduce-scatter.16.cloned.1.call-start = ((), (), s32[]{:S(2)}) async-start(), calls=%async_computation.19 | async-start | bytes 12582912 | tf_op jit(solution)/shard_map/reduce_scatter | solution.py:137
  2213.7 367.9 %all-reduce.7.cloned.1.call-start = ((), (), s32[]{:S(2)}) async-start(), calls=%async_computation.36 | async-start | bytes 4194304 | tf_op jit(solution)/shard_map/psum | solution.py:336
  (45 other events, 610.5 us)
Sparse Core Ops, SparseCore 0:
  10.2 47.8 all-gather.32
  59.7 55.5 all-gather.30
  117.5 37.9 all-gather.34
  330.6 10.3 reduce-scatter.21
  343.1 99.2 reduce-scatter.19
  444.7 50.7 all-gather.38
  497.0 55.2 all-gather.36
  553.9 56.7 all-gather.28
  613.1 50.5 all-gather.26
  694.4 8.7 reduce-scatter.25
  709.1 97.7 reduce-scatter.23
  817.3 56.7 all-gather.40
  1530.6 10.2 reduce-scatter.29
  1543.1 99.2 reduce-scatter.27
  1644.6 45.2 all-gather.16
  1691.9 55.6 all-gather.14
  1749.8 37.8 all-gather.18
  1911.1 10.1 reduce-scatter.13
  1923.6 99.2 reduce-scatter.11
  2025.6 10.2 reduce-scatter.31
  2038.0 50.6 all-gather.22
  2090.9 55.2 all-gather.20
  2148.3 50.7 all-gather.24
  2202.5 61.9 all-reduce.8
  2270.0 95.9 all-reduce.10
  2368.7 9.0 reduce-scatter.17
  2380.0 99.2 reduce-scatter.15
  2483.2 98.2 all-reduce.6
